TPU v7x, 32 devices: a whole 2x2x4 slice. The times are simulated.
32 devices in a mesh: tab: 8 (over z, x), blk: 4 (over y, core).
Axes of the slice: x: 2, y: 2, z: 4, core: 2. Of those that a mesh axis runs over, the one named last changes fastest.
Arguments:
- tables: bfloat16 [64, 512, 768], P('tab', 'blk'), may hold values from -6 to 6
- lengths: int32 [64], P('tab'), may hold values from 60 to 512, as said below
- cotangent: bfloat16 [64, 512, 768], P('tab', 'blk'), may hold values from -6 to 6
- step_count: int32 [1], replicated, may hold values from 2 to 20
- w_qkv: float32 [768, 2304], P('tab'), may hold values from -0.21875 to 0.21875
- w_out: float32 [768, 768], P('tab'), may hold values from -3.5 to 3.5
- w_up: float32 [768, 3072], P('tab'), may hold values from -0.21875 to 0.21875
- w_down: float32 [3072, 768], P('tab'), may hold values from -0.109375 to 0.109375
- vectors: float32 [768, 12], P('tab')
- first_qkv: float32 [768, 2304], P('tab'), may hold values from -128 to 128
- first_out: float32 [768, 768], P('tab'), may hold values from -12 to 12
- first_up: float32 [768, 3072], P('tab'), may hold values from -80 to 80
- first_down: float32 [3072, 768], P('tab'), may hold values from -64 to 64
- first_vec: float32 [768, 12], P('tab'), may hold values from -128 to 128
- second_qkv: float32 [768, 2304], P('tab'), may hold values from 16.384 to 262.144
- second_out: float32 [768, 768], P('tab'), may hold values from 0.16384 to 2.62144
- second_up: float32 [768, 3072], P('tab'), may hold values from 8.192 to 131.072
- second_down: float32 [3072, 768], P('tab'), may hold values from 5.89824 to 95.0272
- second_vec: float32 [768, 12], P('tab'), may hold values from 16.384 to 262.144
Outputs:
- output: bfloat16 [64, 512, 768], P('tab', 'blk')
- grad_input: float32 [64, 512, 768], P('tab', 'blk')
- moment_qkv: float32 [768, 2304], P('tab')
- square_qkv: float32 [768, 2304], P('tab')
- master_qkv: float32 [768, 2304], P('tab')
- copy_qkv: bfloat16 [768, 2304], P('tab')
- moment_out: float32 [768, 768], P('tab')
- square_out: float32 [768, 768], P('tab')
- master_out: float32 [768, 768], P('tab')
- copy_out: bfloat16 [768, 768], P('tab')
- moment_up: float32 [768, 3072], P('tab')
- square_up: float32 [768, 3072], P('tab')
- master_up: float32 [768, 3072], P('tab')
- copy_up: bfloat16 [768, 3072], P('tab')
- moment_down: float32 [3072, 768], P('tab')
- square_down: float32 [3072, 768], P('tab')
- master_down: float32 [3072, 768], P('tab')
- copy_down: bfloat16 [3072, 768], P('tab')
- moment_vec: float32 [768, 12], P('tab')
- square_vec: float32 [768, 12], P('tab')
- master_vec: float32 [768, 12], P('tab')
- copy_vec: bfloat16 [768, 12], P('tab')
Inputs may be any that keep to these rules, and one draw needn't show every extreme that they name: `lengths`: positions from a table's length on are padding; some table has exactly 512 live tokens.
All inputs are finite; a program needn't handle non-finite values.
Results may differ from a plain program's by a relative error of at most 0.018.
Values may be sent and summed in bfloat16 or wider, within the bound.
A program may use at most 256 MiB of HBM per device.

v0:
```python
from functools import partial
import jax
import jax.numpy as jnp
from jax import lax
from jax.sharding import PartitionSpec as P

D = 768
H = 12
HD = 64
LEN = 512
EPS = 1e-06
NEGATIVE = -1e30
BETA_ONE = 0.9
BETA_TWO = 0.999
ADAM_EPS = 1e-08
DECAY = 0.01
RATES = (1.0, 15.0, 1.0, 0.5, 5.0)


def layer_norm(hidden, gain_vec, shift_vec):
    row_mean = jnp.mean(hidden, axis=-1, keepdims=True)
    centred = hidden - row_mean
    variance = jnp.mean(centred * centred, axis=-1, keepdims=True)
    return centred * lax.rsqrt(variance + EPS) * gain_vec + shift_vec


def inner(left, right):
    return lax.dot_general(
        left, right, (((0,), (0,)), ((), ())), preferred_element_type=jnp.float32
    )


def back_mul(left, right):
    return lax.dot_general(
        left, right, (((1,), (1,)), ((), ())), preferred_element_type=jnp.float32
    )


def adam(master, gradient, first_moment, second_moment, rate_now, step_float):
    moment_new = BETA_ONE * first_moment + (1.0 - BETA_ONE) * gradient
    square_new = BETA_TWO * second_moment + (1.0 - BETA_TWO) * gradient * gradient
    fix_one = 1.0 - jnp.power(BETA_ONE, step_float)
    fix_two = 1.0 - jnp.power(BETA_TWO, step_float)
    update = moment_new / fix_one / (jnp.sqrt(square_new / fix_two) + ADAM_EPS)
    master_new = master - rate_now * (update + DECAY * master)
    return (moment_new, square_new, master_new, master_new.astype(jnp.bfloat16))


def local(
    tables,
    lengths,
    cotangent,
    step_count,
    w_qkv,
    w_out,
    w_up,
    w_down,
    vectors,
    first_qkv,
    first_out,
    first_up,
    first_down,
    first_vec,
    second_qkv,
    second_out,
    second_up,
    second_down,
    second_vec,
):
    masters = (w_qkv, w_out, w_up, w_down, vectors)
    firsts = (first_qkv, first_out, first_up, first_down, first_vec)
    seconds = (second_qkv, second_out, second_up, second_down, second_vec)
    full_qkv, full_out, full_up, full_down, full_vec = (
        lax.all_gather(w_qkv.astype(jnp.bfloat16), "tab", axis=0, tiled=True),
        lax.all_gather(w_out.astype(jnp.bfloat16), "tab", axis=0, tiled=True),
        lax.all_gather(w_up.astype(jnp.bfloat16), "tab", axis=0, tiled=True),
        lax.all_gather(w_down.astype(jnp.bfloat16), "tab", axis=0, tiled=True),
        lax.all_gather(vectors.astype(jnp.bfloat16), "tab", axis=0, tiled=True),
    )
    vec_f = full_vec.astype(jnp.float32)
    bias_up = vec_f[:, 8:12].T.reshape(-1)
    table_count = tables.shape[0]
    local_len = tables.shape[1]
    scale_q = HD ** (-0.5)
    valid_keys = (
        lax.broadcasted_iota(jnp.int32, (table_count, 1, 1, LEN), 3) < lengths[:, None, None, None]
    )

    def score_block(query_h, key_h):
        raw_scores = (
            jnp.einsum("bqhd,bkhd->bhqk", query_h, key_h, preferred_element_type=jnp.float32)
            * scale_q
        )
        return jnp.where(valid_keys, raw_scores, NEGATIVE)

    tok_rows = tables.reshape(-1, D)
    proj_qkv = jnp.dot(tok_rows, full_qkv, preferred_element_type=jnp.float32)
    query_b = (proj_qkv[:, :D] + vec_f[:, 0]).astype(jnp.bfloat16)
    key_loc = proj_qkv[:, D : 2 * D].astype(jnp.bfloat16).reshape(table_count, local_len, D)
    value_loc = (
        (proj_qkv[:, 2 * D :] + vec_f[:, 1]).astype(jnp.bfloat16).reshape(table_count, local_len, D)
    )
    key_all, value_all = (
        lax.all_gather(key_loc, "blk", axis=1, tiled=True),
        lax.all_gather(value_loc, "blk", axis=1, tiled=True),
    )
    query_h = query_b.reshape(table_count, local_len, H, HD)
    key_h = key_all.reshape(table_count, LEN, H, HD)
    value_h = value_all.reshape(table_count, LEN, H, HD)
    scores = score_block(query_h, key_h)
    row_top = jnp.max(scores, axis=-1, keepdims=True)
    exp_scores = jnp.exp(scores - row_top)
    row_total = jnp.sum(exp_scores, axis=-1, keepdims=True)
    log_total = row_top + jnp.log(row_total)
    probs_b = (exp_scores / row_total).astype(jnp.bfloat16)
    mixed_heads = jnp.einsum(
        "bhqk,bkhd->bqhd", probs_b, value_h, preferred_element_type=jnp.float32
    )
    mixed_heads = mixed_heads.reshape(-1, D).astype(jnp.bfloat16)
    attn_out = jnp.dot(mixed_heads, full_out, preferred_element_type=jnp.float32) + vec_f[:, 2]
    normed_one, norm_one_back = jax.vjp(
        layer_norm, tok_rows.astype(jnp.float32) + attn_out, vec_f[:, 4], vec_f[:, 5]
    )
    normed_b = normed_one.astype(jnp.bfloat16)
    hidden = jnp.dot(normed_b, full_up, preferred_element_type=jnp.float32) + bias_up
    active, gelu_back = jax.vjp(partial(jax.nn.gelu, approximate=False), hidden)
    active_b = active.astype(jnp.bfloat16)
    branch = jnp.dot(active_b, full_down, preferred_element_type=jnp.float32) + vec_f[:, 3]
    result, norm_two_back = jax.vjp(layer_norm, normed_one + branch, vec_f[:, 6], vec_f[:, 7])
    output = result.astype(jnp.bfloat16).reshape(tables.shape)
    grad_out = cotangent.reshape(-1, D).astype(jnp.float32)
    grad_two, grad_g2, grad_c2 = norm_two_back(grad_out)
    grad_b2 = jnp.sum(grad_two, axis=0)
    branch_b = grad_two.astype(jnp.bfloat16)
    gw_down = inner(active_b, branch_b)
    grad_hidden = gelu_back(back_mul(branch_b, full_down))[0]
    grad_b1 = jnp.sum(grad_hidden, axis=0)
    hidden_b = grad_hidden.astype(jnp.bfloat16)
    gw_up = inner(normed_b, hidden_b)
    grad_one, grad_g1, grad_c1 = norm_one_back(grad_two + back_mul(hidden_b, full_up))
    grad_bo = jnp.sum(grad_one, axis=0)
    attn_b = grad_one.astype(jnp.bfloat16)
    gw_out = inner(mixed_heads, attn_b)
    grad_mixed = (
        back_mul(attn_b, full_out).astype(jnp.bfloat16).reshape(table_count, local_len, H, HD)
    )
    key_back, value_back = (
        lax.all_gather(key_loc, "blk", axis=1, tiled=True),
        lax.all_gather(value_loc, "blk", axis=1, tiled=True),
    )
    key_again = key_back.reshape(table_count, LEN, H, HD)
    value_again = value_back.reshape(table_count, LEN, H, HD)
    probs_again = jnp.exp(score_block(query_h, key_again) - log_total)
    grad_probs = jnp.einsum(
        "bqhd,bkhd->bhqk", grad_mixed, value_again, preferred_element_type=jnp.float32
    )
    row_dot = jnp.sum(grad_probs * probs_again, axis=-1, keepdims=True)
    grad_scores = (probs_again * (grad_probs - row_dot)).astype(jnp.bfloat16)
    grad_query = (
        jnp.einsum(
            "bhqk,bkhd->bqhd", grad_scores, key_again, preferred_element_type=jnp.float32
        ).reshape(-1, D)
        * scale_q
    )
    probs_again_b = probs_again.astype(jnp.bfloat16)
    part_key = (
        jnp.einsum(
            "bhqk,bqhd->bkhd", grad_scores, query_h, preferred_element_type=jnp.float32
        ).reshape(table_count, LEN, D)
        * scale_q
    )
    part_value = jnp.einsum(
        "bhqk,bqhd->bkhd", probs_again_b, grad_mixed, preferred_element_type=jnp.float32
    ).reshape(table_count, LEN, D)
    grad_key, grad_value = (
        lax.psum_scatter(
            part_key.astype(jnp.bfloat16), "blk", scatter_dimension=1, tiled=True
        ).astype(jnp.float32),
        lax.psum_scatter(
            part_value.astype(jnp.bfloat16), "blk", scatter_dimension=1, tiled=True
        ).astype(jnp.float32),
    )
    grad_key = grad_key.reshape(-1, D)
    grad_value = grad_value.reshape(-1, D)
    grad_bq = jnp.sum(grad_query, axis=0)
    grad_bv = jnp.sum(grad_value, axis=0)
    grad_qkv = jnp.concatenate([grad_query, grad_key, grad_value], axis=1).astype(jnp.bfloat16)
    gw_qkv = inner(tok_rows, grad_qkv)
    grad_input = grad_one + back_mul(grad_qkv, full_qkv)
    gw_vec = jnp.concatenate(
        [
            jnp.stack(
                [grad_bq, grad_bv, grad_bo, grad_b2, grad_g1, grad_c1, grad_g2, grad_c2], axis=1
            ),
            grad_b1.reshape(4, D).T,
        ],
        axis=1,
    )
    share_qkv, share_out, share_up, share_down, share_vec = (
        lax.psum_scatter(gw_qkv, "tab", scatter_dimension=0, tiled=True),
        lax.psum_scatter(gw_out, "tab", scatter_dimension=0, tiled=True),
        lax.psum_scatter(gw_up, "tab", scatter_dimension=0, tiled=True),
        lax.psum_scatter(gw_down, "tab", scatter_dimension=0, tiled=True),
        lax.psum_scatter(gw_vec, "tab", scatter_dimension=0, tiled=True),
    )
    shares = (
        lax.psum(share_qkv.astype(jnp.bfloat16), "blk").astype(jnp.float32),
        lax.psum(share_out.astype(jnp.bfloat16), "blk").astype(jnp.float32),
        lax.psum(share_up.astype(jnp.bfloat16), "blk").astype(jnp.float32),
        lax.psum(share_down.astype(jnp.bfloat16), "blk").astype(jnp.float32),
        lax.psum(share_vec.astype(jnp.bfloat16), "blk").astype(jnp.float32),
    )
    step_float = step_count[0].astype(jnp.float32)
    results = [output, grad_input.reshape(tables.shape)]
    for position in range(5):
        results.extend(
            adam(
                masters[position],
                shares[position],
                firsts[position],
                seconds[position],
                RATES[position],
                step_float,
            )
        )
    return tuple(results)


def solution(mesh):
    return jax.shard_map(
        local,
        mesh=mesh,
        in_specs=(
            P("tab", "blk", None),
            P("tab"),
            P("tab", "blk", None),
            P(),
            P("tab", None),
            P("tab", None),
            P("tab", None),
            P("tab", None),
            P("tab", None),
            P("tab", None),
            P("tab", None),
            P("tab", None),
            P("tab", None),
            P("tab", None),
            P("tab", None),
            P("tab", None),
            P("tab", None),
            P("tab", None),
            P("tab", None),
        ),
        out_specs=(
            P("tab", "blk", None),
            P("tab", "blk", None),
            P("tab", None),
            P("tab", None),
            P("tab", None),
            P("tab", None),
            P("tab", None),
            P("tab", None),
            P("tab", None),
            P("tab", None),
            P("tab", None),
            P("tab", None),
            P("tab", None),
            P("tab", None),
            P("tab", None),
            P("tab", None),
            P("tab", None),
            P("tab", None),
            P("tab", None),
            P("tab", None),
            P("tab", None),
            P("tab", None),
        ),
        check_vma=False,
    )
```

profile of v0, /device:TPU:0, one launch (start us, length us, event | category | flops | bytes accessed | tf_op | source)
XLA Modules:
  0.0 1251.9 jit_solution(16198308453331200462)
XLA Ops:
  9.3 68.8 %all-gather.8.cloned.1.call-done = bf16[768,2304]{1,0:T(8,128)(2,1)} async-done(((bf16[96,2304]{1,0:T(8,128)(2,1)}), bf16[768,2304]{1,0:T(8,128)(2,1)}) %all-gather.8.cloned.1.call-update) | async-done | bytes 3538960 | tf_op jit(solution)/shard_map/all_gather | solution.py:74
  89.4 30.6 %all-gather = bf16[8,96,12]{1,2,0:T(8,128)(2,1)S(1)} all-gather(bf16[1,96,12]{1,2,0:T(8,128)(2,1)S(1)} %convert_bitcast_fusion), channel_id=1, replica_groups=mesh['tab'=8,'blk'=4] {'tab'}, dimensions={0}, use_global_device_ids=true | all-gather | bytes 20736 | tf_op jit(solution)/shard_map/all_gather | solution.py:78
  143.3 12.9 %fusion.12 = (f32[8,12,128]{2,1,0:T(8,128)S(1)}, f32[8,12,128,512]{3,2,1,0:T(8,128)}) fusion(pred[8,512]{1,0:T(8,128)(4,1)S(1)} %iota_compare_fusion, bf16[8,512,12,64]{1,3,2,0:T(8,128)(2,1)} %bitcast.94, bf16[8,128,12,64]{1,0,3,2:T(8,128)(2,1)S(1)} %bitcast.99), kind=kOutput, calls=%fused_computation.29 | convolution fusion | flops 824168448 | bytes 33083392 | tf_op jit(solution)/shard_map/bqhd,bkhd->bhqk/dot_general | solution.py:91
  156.1 11.6 fusion
  168.4 14.7 %all-gather.10.cloned.1.call-done = bf16[8,512,768]{2,1,0:T(8,128)(2,1)} async-done(((bf16[8,128,768]{2,1,0:T(8,128)(2,1)}), bf16[8,512,768]{2,1,0:T(8,128)(2,1)}) %all-gather.10.cloned.1.call-update) | async-done | bytes 6291472 | tf_op jit(solution)/shard_map/all_gather | solution.py:105
  191.8 13.4 %fusion.35 = bf16[8,128,12,64]{1,3,2,0:T(8,128)(2,1)S(1)} fusion(bf16[8,512,12,64]{1,3,2,0:T(8,128)(2,1)} %bitcast.97, f32[8,12,128]{2,1,0:T(8,128)S(1)} %fusion, f32[8,12,128]{2,1,0:T(8,128)S(1)} %get-tuple-element.136, f32[8,12,128,512]{3,2,1,0:T(8,128)} %get-tuple-element.137, pred[8,512]{1,0:T(8,128)(4,1)S(1)} %iota_compare_fusion), kind=kOutput, calls=%fused_computation.79 | convolution fusion | flops 837550080 | bytes 33132544 | tf_op jit(solution)/shard_map/bhqk,bkhd->bqhd/dot_general | solution.py:116
  207.6 19.3 %all-gather.14.cloned.1.call-done = bf16[768,768]{1,0:T(8,128)(2,1)} async-done(((bf16[96,768]{1,0:T(8,128)(2,1)}), bf16[768,768]{1,0:T(8,128)(2,1)}) %all-gather.14.cloned.1.call-update) | async-done | bytes 1179664 | tf_op jit(solution)/shard_map/all_gather | solution.py:75
  231.3 76.3 %all-gather.16.cloned.1.call-done = bf16[768,3072]{1,0:T(8,128)(2,1)} async-done(((bf16[96,3072]{1,0:T(8,128)(2,1)}), bf16[768,3072]{1,0:T(8,128)(2,1)}) %all-gather.16.cloned.1.call-update) | async-done | bytes 4718608 | tf_op jit(solution)/shard_map/all_gather | solution.py:76
  307.6 36.0 %multiply_convert_fusion.2 = (bf16[1024,3072]{1,0:T(8,128)(2,1)}, f32[1024,3072]{1,0:T(8,128)}, f32[1024,3072]{1,0:T(8,128)}) fusion(f32[3072]{0:T(1024)S(1)} %add.223, bf16[768,3072]{1,0:T(8,128)(2,1)} %all-gather.16.cloned.1.call-done, f32[1024,768]{1,0:T(8,128)S(1)} %get-tuple-element.139, f32[768]{0:T(1024)S(1)} %get-tuple-element.96, ...), kind=kOutput, calls=%fused_computation.14 | convolution fusion | flops 5043388416 | bytes 39348224 | tf_op jit(solution)/shard_map/dot_general | solution.py:125
  343.6 44.3 %all-gather.18.cloned.1.call-done = bf16[3072,768]{1,0:T(8,128)(2,1)} async-done(((bf16[384,768]{1,0:T(8,128)(2,1)}), bf16[3072,768]{1,0:T(8,128)(2,1)}) %all-gather.18.cloned.1.call-update) | async-done | bytes 4718608 | tf_op jit(solution)/shard_map/all_gather | solution.py:77
  403.0 19.2 %fusion.86 = (f32[3072]{0:T(1024)S(1)}, bf16[1024,3072]{1,0:T(8,128)(2,1)}) fusion(f32[1024,3072]{1,0:T(8,128)} %get-tuple-element.130, bf16[3072,768]{1,0:T(8,128)(2,1)} %all-gather.18.cloned.1.call-done, f32[1024,768]{1,0:T(8,128)} %get-tuple-element.128, f32[1024]{0:T(1024)S(1)} %negate_multiply_fusion.2, f32[1024,3072]{1,0:T(8,128)} %get-tuple-element.140, ...), kind=kOutput, calls=%fused_computation.151 | convolution fusion | flops 4883739648 | bytes 39350272 | tf_op jit(solution)/shard_map/dot_general | solution.py:34
  442.5 13.1 %fusion.13 = bf16[8,12,64,512]{3,2,1,0:T(8,128)(2,1)} fusion(f32[8,12,128]{2,1,0:T(8,128)S(1)} %copy-done.24, f32[8,12,128,512]{3,2,1,0:T(8,128)} %get-tuple-element.137, pred[8,512]{1,0:T(8,128)(4,1)S(1)} %copy-done.26, bf16[8,128,12,64]{1,0,3,2:T(8,128)(2,1)S(1)} %bitcast.108), kind=kOutput, calls=%fused_computation.34 | convolution fusion | flops 833617920 | bytes 33083392 | tf_op jit(solution)/shard_map/bhqk,bqhd->bkhd/dot_general | solution.py:172
  464.3 24.1 %multiply_reduce_fusion = (f32[8,12,128]{2,1,0:T(8,128)S(1)}, f32[8,12,128,512]{3,2,1,0:T(8,128)}) fusion(f32[8,12,128]{2,1,0:T(8,128)S(1)} %copy-done.24, f32[8,12,128,512]{3,2,1,0:T(8,128)} %get-tuple-element.137, pred[8,512]{1,0:T(8,128)(4,1)S(1)} %copy-done.26, bf16[8,512,12,64]{1,3,2,0:T(8,128)(2,1)} %bitcast.98, bf16[8,128,12,64]{1,0,3,2:T(8,128)(2,1)} %bitcast.109), kind=kOutput, calls=%fused_computation.1 | convolution fusion | flops 836751360 | bytes 58298368 | tf_op jit(solution)/shard_map/bqhd,bkhd->bhqk/dot_general | solution.py:154
  488.5 17.0 %multiply_convert_fusion = bf16[8,12,128,512]{3,2,1,0:T(8,128)(2,1)S(1)} fusion(f32[8,12,128,512]{3,2,1,0:T(8,128)} %get-tuple-element.145, f32[8,12,128]{2,1,0:T(8,128)S(1)} %get-tuple-element.144, f32[8,12,128]{2,1,0:T(8,128)S(1)} %copy-done.24, f32[8,12,128,512]{3,2,1,0:T(8,128)} %get-tuple-element.137, pred[8,512]{1,0:T(8,128)(4,1)S(1)} %copy-done.26), kind=kLoop, calls=%fused_computation | loop fusion | flops 37748736 | bytes 63016960 | tf_op jit(solution)/shard_map/convert_element_type | solution.py:158
  526.2 10.8 fusion.22
  538.9 10.8 fusion.62
  550.0 10.8 multiply_reduce_fusion.5
  564.9 18.2 %reduce-scatter.12.cloned.1.call-done = bf16[8,128,768]{2,1,0:T(8,128)(2,1)} async-done(((bf16[8,512,768]{2,1,0:T(8,128)(2,1)}), bf16[8,128,768]{2,1,0:T(8,128)(2,1)}) %reduce-scatter.12.cloned.1.call-update) | async-done | bytes 1572880 | tf_op jit(solution)/shard_map/reduce_scatter | solution.py:176
  611.2 45.1 %reduce-scatter.16.cloned.1.call-done = f32[96,768]{1,0:T(8,128)} async-done(((f32[768,768]{1,0:T(8,128)}), f32[96,768]{1,0:T(8,128)}) %reduce-scatter.16.cloned.1.call-update) | async-done | bytes 294928 | tf_op jit(solution)/shard_map/reduce_scatter | solution.py:201
  657.9 163.1 %reduce-scatter.18.cloned.1.call-done = f32[96,3072]{1,0:T(8,128)} async-done(((f32[768,3072]{1,0:T(8,128)}), f32[96,3072]{1,0:T(8,128)}) %reduce-scatter.18.cloned.1.call-update) | async-done | bytes 1179664 | tf_op jit(solution)/shard_map/reduce_scatter | solution.py:202
  823.2 162.7 %reduce-scatter.20.cloned.1.call-done = f32[384,768]{1,0:T(8,128)} async-done(((f32[3072,768]{1,0:T(8,128)}), f32[384,768]{1,0:T(8,128)}) %reduce-scatter.20.cloned.1.call-update) | async-done | bytes 1179664 | tf_op jit(solution)/shard_map/reduce_scatter | solution.py:203
  988.0 130.0 %reduce-scatter.22.cloned.1.call-done = f32[96,2304]{1,0:T(8,128)} async-done(((f32[768,2304]{1,0:T(8,128)}), f32[96,2304]{1,0:T(8,128)}) %reduce-scatter.22.cloned.1.call-update) | async-done | bytes 884752 | tf_op jit(solution)/shard_map/reduce_scatter | solution.py:200
  1129.4 53.9 %reduce-scatter.24.cloned.1.call-done = f32[96,12]{1,0:T(8,128)} async-done(((f32[768,12]{1,0:T(8,128)}), f32[96,12]{1,0:T(8,128)}) %reduce-scatter.24.cloned.1.call-update) | async-done | bytes 4624
  1190.5 42.2 %all-reduce.3.cloned.1.call-done = (bf16[96,2304]{1,0:T(8,128)(2,1)}, bf16[96,768]{1,0:T(8,128)(2,1)}, bf16[96,3072]{1,0:T(8,128)(2,1)}, bf16[384,768]{1,0:T(8,128)(2,1)}) async-done(((bf16[96,2304]{1,0:T(8,128)(2,1)}, bf16[96,768]{1,0:T(8,128)(2,1)}, bf16[96,3072]{1,0:T(8,128)(2,1)}, bf16[384,768]{1,0:T(8,128)(2,1)}), (bf16[96,2304]{1,0:T(8,128)(2,1)}, bf16[96,768]{1,0:T(8,128)(2,1)}, ...) | async-done | bytes 1769488 | tf_op jit(solution)/shard_map/psum | solution.py:207
  (180 shorter events, 187.3 us)
Async XLA Ops:
  7.2 70.9 %all-gather.8.cloned.1.call-start = ((), (), s32[]{:S(2)}) async-start(), calls=%async_computation.7 | async-start | bytes 3981312 | tf_op jit(solution)/shard_map/all_gather | solution.py:74
  9.2 125.4 %all-gather.12.cloned.1.call-start = ((), (), s32[]{:S(2)}) async-start(), calls=%async_computation.9 | async-start | bytes 7864320 | tf_op jit(solution)/shard_map/all_gather | solution.py:104
  89.4 93.8 %all-gather.10.cloned.1.call-start = ((), (), s32[]{:S(2)}) async-start(), calls=%async_computation.8 | async-start | bytes 7864320 | tf_op jit(solution)/shard_map/all_gather | solution.py:105
  125.5 101.4 %all-gather.14.cloned.1.call-start = ((), (), s32[]{:S(2)}) async-start(), calls=%async_computation.10 | async-start | bytes 1327104 | tf_op jit(solution)/shard_map/all_gather | solution.py:75
  126.2 181.3 %all-gather.16.cloned.1.call-start = ((), (), s32[]{:S(2)}) async-start(), calls=%async_computation.11 | async-start | bytes 5308416 | tf_op jit(solution)/shard_map/all_gather | solution.py:76
  127.2 260.7 %all-gather.18.cloned.1.call-start = ((), (), s32[]{:S(2)}) async-start(), calls=%async_computation.12 | async-start | bytes 5308416 | tf_op jit(solution)/shard_map/all_gather | solution.py:77
  129.4 433.2 %reduce-scatter.14.cloned.1.call-start = ((), (), s32[]{:S(2)}) async-start(), calls=%async_computation.14 | async-start | bytes 7864320 | tf_op jit(solution)/shard_map/reduce_scatter | solution.py:179
  129.7 62.0 %copy-start.25 = (pred[8,512]{1,0:T(8,128)(4,1)}, pred[8,512]{1,0:T(8,128)(4,1)S(1)}, u32[]{:S(2)}) copy-start(pred[8,512]{1,0:T(8,128)(4,1)S(1)} %iota_compare_fusion) | copy-start | bytes 12292
  307.6 80.3 %copy-start.34 = (f32[768]{0:T(1024)S(1)}, f32[768]{0:T(1024)}, u32[]{:S(2)}) copy-start(f32[768]{0:T(1024)} %get-tuple-element.95) | copy-start | bytes 9220
  464.3 118.8 %reduce-scatter.12.cloned.1.call-start = ((), (), s32[]{:S(2)}) async-start(), calls=%async_computation.13 | async-start | bytes 7864320 | tf_op jit(solution)/shard_map/reduce_scatter | solution.py:176
  488.5 17.1 %copy-start.2 = (bf16[96,8,8,128]{3,2,1,0:T(8,128)(2,1)S(1)}, bf16[96,8,8,128]{3,2,1,0:T(8,128)(2,1)}, u32[]{:S(2)}) copy-start(bf16[96,8,8,128]{3,2,1,0:T(8,128)(2,1)} %copy-done.1) | copy-start | bytes 4718596
  520.7 135.6 %reduce-scatter.16.cloned.1.call-start = ((), (), s32[]{:S(2)}) async-start(), calls=%async_computation.15 | async-start | bytes 2654208 | tf_op jit(solution)/shard_map/reduce_scatter | solution.py:201
  526.1 294.9 %reduce-scatter.18.cloned.1.call-start = ((), (), s32[]{:S(2)}) async-start(), calls=%async_computation.16 | async-start | bytes 10616832 | tf_op jit(solution)/shard_map/reduce_scatter | solution.py:202
  537.0 448.9 %reduce-scatter.20.cloned.1.call-start = ((), (), s32[]{:S(2)}) async-start(), calls=%async_computation.17 | async-start | bytes 10616832 | tf_op jit(solution)/shard_map/reduce_scatter | solution.py:203
  549.8 568.3 %reduce-scatter.22.cloned.1.call-start = ((), (), s32[]{:S(2)}) async-start(), calls=%async_computation.18 | async-start | bytes 7962624 | tf_op jit(solution)/shard_map/reduce_scatter | solution.py:200
  562.6 23.2 %copy-start.14 = (bf16[96,8,8,128]{3,1,2,0:T(8,128)(2,1)}, bf16[96,8,8,128]{3,1,2,0:T(8,128)(2,1)S(1)}, u32[]{:S(2)}) copy-start(bf16[96,8,8,128]{3,1,2,0:T(8,128)(2,1)S(1)} %copy.149) | copy-start | bytes 4718596
  564.9 29.5 %copy-start.15 = (bf16[1024,768]{0,1:T(8,128)(2,1)}, bf16[1024,768]{0,1:T(8,128)(2,1)S(1)}, u32[]{:S(2)}) copy-start(bf16[1024,768]{0,1:T(8,128)(2,1)S(1)} %copy.115) | copy-start | bytes 4718596
  602.5 580.8 %reduce-scatter.24.cloned.1.call-start = ((), (), s32[]{:S(2)}) async-start(), calls=%async_computation.19 | async-start | bytes 442368
  610.2 622.5 %all-reduce.3.cloned.1.call-start = ((), (), s32[]{:S(2)}) async-start(), calls=%async_computation.20 | async-start | bytes 3538944 | tf_op jit(solution)/shard_map/psum | solution.py:207
  657.9 462.2 %copy-start.6 = (f32[1024,768]{1,0:T(8,128)S(1)}, f32[1024,768]{1,0:T(8,128)}, u32[]{:S(2)}) copy-start(f32[1024,768]{1,0:T(8,128)} %copy-done.5) | copy-start | bytes 9437188
  1120.1 69.7 %copy-start.29 = (f32[96,12]{0,1:T(8,128)S(1)}, f32[96,12]{0,1:T(8,128)}, u32[]{:S(2)}) copy-start(f32[96,12]{0,1:T(8,128)} %param.27) | copy-start | bytes 13828
  1120.1 69.7 %copy-start.32 = (f32[96,12]{0,1:T(8,128)S(1)}, f32[96,12]{0,1:T(8,128)}, u32[]{:S(2)}) copy-start(f32[96,12]{0,1:T(8,128)} %param.37) | copy-start | bytes 13828
  1120.1 69.7 %copy-start.33 = (f32[96,12]{0,1:T(8,128)S(1)}, f32[96,12]{0,1:T(8,128)}, u32[]{:S(2)}) copy-start(f32[96,12]{0,1:T(8,128)} %param.32) | copy-start | bytes 13828
  1120.1 112.5 %copy-start.21 = (f32[96,768]{1,0:T(8,128)S(1)}, f32[96,768]{1,0:T(8,128)}, u32[]{:S(2)}) copy-start(f32[96,768]{1,0:T(8,128)} %param.24) | copy-start | bytes 884740
  (27 other events, 106.9 us)
Sparse Core Ops, SparseCore 0:
  10.8 67.3 all-gather.7
  89.5 45.0 all-gather.11
  136.8 46.3 all-gather.9
  185.8 41.1 all-gather.13
  229.5 77.9 all-gather.15
  310.2 77.6 all-gather.17
  464.4 57.2 reduce-scatter.13
  524.2 58.8 reduce-scatter.11
  586.6 69.6 reduce-scatter.15
  659.7 161.2 reduce-scatter.17
  824.7 161.2 reduce-scatter.19
  989.4 128.6 reduce-scatter.21
  1121.9 61.3 reduce-scatter.23
  1187.5 45.1 all-reduce.2
where the time goes:
time: 1260 us; the launch traced here: 1250 us
  waiting for transfers between devices  843 us (67%)
  matrix products  210 us (17%)
  local copies, waits for them, and re-layouts  74.5 us (6%)
  other arithmetic  71.6 us (6%)
  blocking collectives  36.3 us (3%)
  between operations  15.5 us (1%)
    reduce_scatter x1, waiting for transfers between devices, local(): lax.psum_scatter(gw_up, 'tab', scatter_dimension=0, tiled=True)  163 us
    reduce_scatter x1, waiting for transfers between devices, local(): lax.psum_scatter(gw_down, 'tab', scatter_dimension=0, tiled=True)  163 us
    reduce_scatter x1, waiting for transfers between devices, local(): lax.psum_scatter(gw_qkv, 'tab', scatter_dimension=0, tiled=True)  130 us
    all_gather x1, waiting for transfers between devices, local(): lax.all_gather(w_up.astype(jnp.bfloat16), 'tab', axis=0, tiled=True)  76.3 us
    all_gather x1, waiting for transfers between devices, local(): lax.all_gather(w_qkv.astype(jnp.bfloat16), 'tab', axis=0, tiled=True)  68.8 us
    unnamed x15, waiting for transfers between devices  54.1 us
    reduce_scatter x1, waiting for transfers between devices, local(): lax.psum_scatter(gw_out, 'tab', scatter_dimension=0, tiled=True)  45.1 us
    all_gather x1, waiting for transfers between devices, local(): lax.all_gather(w_down.astype(jnp.bfloat16), 'tab', axis=0, tiled=True)  44.3 us
  transfers between devices with their start and end apart: 14, of which 13 were waited for; matrix products, arithmetic and copies ran while one was open for 20% of the time, Pallas kernels for 0%

commit v1 on v0

--- a/solution.py
+++ b/solution.py
@@ -15,6 +15,24 @@
 ADAM_EPS = 1e-08
 DECAY = 0.01
 RATES = (1.0, 15.0, 1.0, 0.5, 5.0)
+
+
+def collect(array, axis, dim):
+    ways, here, step = (lax.axis_size(axis), lax.axis_index(axis), array.shape[dim])
+    shape = [n * ways if d == dim else n for d, n in enumerate(array.shape)]
+    full = lax.dynamic_update_slice_in_dim(
+        jnp.zeros(shape, array.dtype), array, here * step, axis=dim
+    )
+    going_up = going_down = array
+    for far in range(1, ways // 2 + 1):
+        going_up = lax.ppermute(going_up, axis, [(d, (d + 1) % ways) for d in range(ways)])
+        full = lax.dynamic_update_slice_in_dim(full, going_up, (here - far) % ways * step, axis=dim)
+        if 2 * far < ways:
+            going_down = lax.ppermute(going_down, axis, [(d, (d - 1) % ways) for d in range(ways)])
+            full = lax.dynamic_update_slice_in_dim(
+                full, going_down, (here + far) % ways * step, axis=dim
+            )
+    return full
 
 
 def layer_norm(hidden, gain_vec, shift_vec):
@@ -71,7 +89,7 @@
     firsts = (first_qkv, first_out, first_up, first_down, first_vec)
     seconds = (second_qkv, second_out, second_up, second_down, second_vec)
     full_qkv, full_out, full_up, full_down, full_vec = (
-        lax.all_gather(w_qkv.astype(jnp.bfloat16), "tab", axis=0, tiled=True),
+        collect(w_qkv.astype(jnp.bfloat16), "tab", 0),
         lax.all_gather(w_out.astype(jnp.bfloat16), "tab", axis=0, tiled=True),
         lax.all_gather(w_up.astype(jnp.bfloat16), "tab", axis=0, tiled=True),
         lax.all_gather(w_down.astype(jnp.bfloat16), "tab", axis=0, tiled=True),

time: 1260 us -> 1270 us (level)
  starting transfers between devices: 1.22 us -> 20.9 us
  waiting for transfers between devices: 843 us -> 824 us
    all_gather x1 -> x0, waiting for transfers between devices: 68.8 us -> none  [local(): lax.all_gather(w_qkv.astype(jnp.bfloat16), 'tab', axis=0, tiled=True)]
    ppermute x0 -> x7, waiting for transfers between devices: none -> 51.2 us  [the longest x4 51.2 us: collect(): lax.ppermute(going_up, axis, [(d, (d + 1) % ways) for d in range(ways)])]
    ppermute x0 -> x7, starting transfers between devices: none -> 19.5 us  [the longest x4 10.4 us: collect(): lax.ppermute(going_up, axis, [(d, (d + 1) % ways) for d in range(ways)])]
    unnamed x80 -> x86, local copies, waits for them, and re-layouts: 25.7 us -> 28.4 us
    unnamed x15 -> x14, waiting for transfers between devices: 54.1 us -> 53.9 us
  transfers between devices with their start and end apart: 14 -> 20, of which waited for: 13 -> 16; matrix products, arithmetic and copies ran while one was open for 20% -> 20% of each run, Pallas kernels for 0% -> 0%
where the time goes in v1:
time: 1270 us; the launch traced here: 1260 us
  waiting for transfers between devices  824 us (65%)
  matrix products  210 us (17%)
  local copies, waits for them, and re-layouts  83 us (7%)
  other arithmetic  69.7 us (5%)
  blocking collectives  36.3 us (3%)
  starting transfers between devices  20.9 us (2%)
  between operations  15.5 us (1%)
    reduce_scatter x1, waiting for transfers between devices, local(): lax.psum_scatter(gw_up, 'tab', scatter_dimension=0, tiled=True)  163 us
    reduce_scatter x1, waiting for transfers between devices, local(): lax.psum_scatter(gw_down, 'tab', scatter_dimension=0, tiled=True)  163 us
    reduce_scatter x1, waiting for transfers between devices, local(): lax.psum_scatter(gw_qkv, 'tab', scatter_dimension=0, tiled=True)  130 us
    all_gather x1, waiting for transfers between devices, local(): lax.all_gather(w_up.astype(jnp.bfloat16), 'tab', axis=0, tiled=True)  76.3 us
    unnamed x14, waiting for transfers between devices  53.9 us
    ppermute x4, waiting for transfers between devices, collect(): lax.ppermute(going_up, axis, [(d, (d + 1) % ways) for d in range(ways)])  51.2 us
    reduce_scatter x1, waiting for transfers between devices, local(): lax.psum_scatter(gw_out, 'tab', scatter_dimension=0, tiled=True)  45 us
    all_gather x1, waiting for transfers between devices, local(): lax.all_gather(w_down.astype(jnp.bfloat16), 'tab', axis=0, tiled=True)  44 us
  transfers between devices with their start and end apart: 20, of which 16 were waited for; matrix products, arithmetic and copies ran while one was open for 20% of the time, Pallas kernels for 0%

profile of v1, /device:TPU:0, one launch (start us, length us, event | category | flops | bytes accessed | tf_op | source)
XLA Modules:
  0.0 1259.6 jit_solution(17961977750830140269)
XLA Ops:
  16.3 15.9 %collective-permute-done = bf16[96,2304]{1,0:T(8,128)(2,1)S(1)} collective-permute-done((bf16[96,2304]{1,0:T(8,128)(2,1)S(1)}, bf16[96,2304]{1,0:T(8,128)(2,1)S(1)}, u32[]{:S(2)}, u32[]{:S(2)}) %collective-permute-start) | collective-permute-done | bytes 442400 | tf_op jit(solution)/shard_map/ppermute | solution.py:28
  39.3 13.4 %collective-permute-done.2 = bf16[96,2304]{1,0:T(8,128)(2,1)S(1)} collective-permute-done((bf16[96,2304]{1,0:T(8,128)(2,1)S(1)}, bf16[96,2304]{1,0:T(8,128)(2,1)S(1)}, u32[]{:S(2)}, u32[]{:S(2)}) %collective-permute-start.2) | collective-permute-done | bytes 442400 | tf_op jit(solution)/shard_map/ppermute | solution.py:28
  59.8 12.7 %collective-permute-done.4 = bf16[96,2304]{1,0:T(8,128)(2,1)S(1)} collective-permute-done((bf16[96,2304]{1,0:T(8,128)(2,1)S(1)}, bf16[96,2304]{1,0:T(8,128)(2,1)S(1)}, u32[]{:S(2)}, u32[]{:S(2)}) %collective-permute-start.4) | collective-permute-done | bytes 442400 | tf_op jit(solution)/shard_map/ppermute | solution.py:28
  97.5 30.6 %all-gather = bf16[8,96,12]{1,2,0:T(8,128)(2,1)S(1)} all-gather(bf16[1,96,12]{1,2,0:T(8,128)(2,1)S(1)} %convert_bitcast_fusion), channel_id=1, replica_groups=mesh['tab'=8,'blk'=4] {'tab'}, dimensions={0}, use_global_device_ids=true | all-gather | bytes 20736 | tf_op jit(solution)/shard_map/all_gather | solution.py:96
  151.1 12.9 %fusion.12 = (f32[8,12,128]{2,1,0:T(8,128)S(1)}, f32[8,12,128,512]{3,2,1,0:T(8,128)}) fusion(pred[8,512]{1,0:T(8,128)(4,1)S(1)} %iota_compare_fusion, bf16[8,512,12,64]{1,3,2,0:T(8,128)(2,1)} %bitcast.96, bf16[8,128,12,64]{1,0,3,2:T(8,128)(2,1)S(1)} %bitcast.101), kind=kOutput, calls=%fused_computation.29 | convolution fusion | flops 824168448 | bytes 33083392 | tf_op jit(solution)/shard_map/bqhd,bkhd->bhqk/dot_general | solution.py:109
  164.0 11.6 fusion
  176.3 14.7 %all-gather.7.cloned.1.call-done = bf16[8,512,768]{2,1,0:T(8,128)(2,1)} async-done(((bf16[8,128,768]{2,1,0:T(8,128)(2,1)}), bf16[8,512,768]{2,1,0:T(8,128)(2,1)}) %all-gather.7.cloned.1.call-update) | async-done | bytes 6291472 | tf_op jit(solution)/shard_map/all_gather | solution.py:123
  199.6 13.4 %fusion.35 = bf16[8,128,12,64]{1,3,2,0:T(8,128)(2,1)S(1)} fusion(bf16[8,512,12,64]{1,3,2,0:T(8,128)(2,1)} %bitcast.99, f32[8,12,128]{2,1,0:T(8,128)S(1)} %fusion, f32[8,12,128]{2,1,0:T(8,128)S(1)} %get-tuple-element.138, f32[8,12,128,512]{3,2,1,0:T(8,128)} %get-tuple-element.139, pred[8,512]{1,0:T(8,128)(4,1)S(1)} %iota_compare_fusion), kind=kOutput, calls=%fused_computation.80 | convolution fusion | flops 837550080 | bytes 33132544 | tf_op jit(solution)/shard_map/bhqk,bkhd->bqhd/dot_general | solution.py:134
  215.5 19.5 %all-gather.11.cloned.1.call-done = bf16[768,768]{1,0:T(8,128)(2,1)} async-done(((bf16[96,768]{1,0:T(8,128)(2,1)}), bf16[768,768]{1,0:T(8,128)(2,1)}) %all-gather.11.cloned.1.call-update) | async-done | bytes 1179664 | tf_op jit(solution)/shard_map/all_gather | solution.py:93
  239.3 76.3 %all-gather.13.cloned.1.call-done = bf16[768,3072]{1,0:T(8,128)(2,1)} async-done(((bf16[96,3072]{1,0:T(8,128)(2,1)}), bf16[768,3072]{1,0:T(8,128)(2,1)}) %all-gather.13.cloned.1.call-update) | async-done | bytes 4718608 | tf_op jit(solution)/shard_map/all_gather | solution.py:94
  315.6 36.3 %multiply_convert_fusion.2 = (bf16[1024,3072]{1,0:T(8,128)(2,1)}, f32[1024,3072]{1,0:T(8,128)}, f32[1024,3072]{1,0:T(8,128)}) fusion(f32[3072]{0:T(1024)S(1)} %add.300, bf16[768,3072]{1,0:T(8,128)(2,1)} %all-gather.13.cloned.1.call-done, f32[1024,768]{1,0:T(8,128)S(1)} %get-tuple-element.141, f32[768]{0:T(1024)S(1)} %get-tuple-element.96, ...), kind=kOutput, calls=%fused_computation.14 | convolution fusion | flops 5043388416 | bytes 39348224 | tf_op jit(solution)/shard_map/dot_general | solution.py:143
  351.9 44.0 %all-gather.15.cloned.1.call-done = bf16[3072,768]{1,0:T(8,128)(2,1)} async-done(((bf16[384,768]{1,0:T(8,128)(2,1)}), bf16[3072,768]{1,0:T(8,128)(2,1)}) %all-gather.15.cloned.1.call-update) | async-done | bytes 4718608 | tf_op jit(solution)/shard_map/all_gather | solution.py:95
  411.0 19.0 %fusion.86 = (f32[3072]{0:T(1024)S(1)}, bf16[1024,3072]{1,0:T(8,128)(2,1)}) fusion(f32[1024,3072]{1,0:T(8,128)} %get-tuple-element.130, bf16[3072,768]{1,0:T(8,128)(2,1)} %all-gather.15.cloned.1.call-done, f32[1024,768]{1,0:T(8,128)} %get-tuple-element.128, f32[1024]{0:T(1024)S(1)} %negate_multiply_fusion.2, f32[1024,3072]{1,0:T(8,128)} %get-tuple-element.142, ...), kind=kOutput, calls=%fused_computation.160 | convolution fusion | flops 4883739648 | bytes 39350272 | tf_op jit(solution)/shard_map/dot_general | solution.py:52
  450.3 13.1 %fusion.13 = bf16[8,12,64,512]{3,2,1,0:T(8,128)(2,1)} fusion(f32[8,12,128]{2,1,0:T(8,128)S(1)} %copy-done.26, f32[8,12,128,512]{3,2,1,0:T(8,128)} %get-tuple-element.139, pred[8,512]{1,0:T(8,128)(4,1)S(1)} %copy-done.28, bf16[8,128,12,64]{1,0,3,2:T(8,128)(2,1)S(1)} %bitcast.110), kind=kOutput, calls=%fused_computation.35 | convolution fusion | flops 833617920 | bytes 33083392 | tf_op jit(solution)/shard_map/bhqk,bqhd->bkhd/dot_general | solution.py:190
  472.1 24.2 %multiply_reduce_fusion = (f32[8,12,128]{2,1,0:T(8,128)S(1)}, f32[8,12,128,512]{3,2,1,0:T(8,128)}) fusion(f32[8,12,128]{2,1,0:T(8,128)S(1)} %copy-done.26, f32[8,12,128,512]{3,2,1,0:T(8,128)} %get-tuple-element.139, pred[8,512]{1,0:T(8,128)(4,1)S(1)} %copy-done.28, bf16[8,512,12,64]{1,3,2,0:T(8,128)(2,1)} %bitcast.100, bf16[8,128,12,64]{1,0,3,2:T(8,128)(2,1)} %bitcast.111), kind=kOutput, calls=%fused_computation.1 | convolution fusion | flops 836751360 | bytes 58298368 | tf_op jit(solution)/shard_map/bqhd,bkhd->bhqk/dot_general | solution.py:172
  496.3 17.0 %multiply_convert_fusion = bf16[8,12,128,512]{3,2,1,0:T(8,128)(2,1)S(1)} fusion(f32[8,12,128,512]{3,2,1,0:T(8,128)} %get-tuple-element.147, f32[8,12,128]{2,1,0:T(8,128)S(1)} %get-tuple-element.146, f32[8,12,128]{2,1,0:T(8,128)S(1)} %copy-done.26, f32[8,12,128,512]{3,2,1,0:T(8,128)} %get-tuple-element.139, pred[8,512]{1,0:T(8,128)(4,1)S(1)} %copy-done.28), kind=kLoop, calls=%fused_computation | loop fusion | flops 37748736 | bytes 63016960 | tf_op jit(solution)/shard_map/convert_element_type | solution.py:176
  558.0 10.8 multiply_reduce_fusion.5
  572.9 18.0 %reduce-scatter.12.cloned.1.call-done = bf16[8,128,768]{2,1,0:T(8,128)(2,1)} async-done(((bf16[8,512,768]{2,1,0:T(8,128)(2,1)}), bf16[8,128,768]{2,1,0:T(8,128)(2,1)}) %reduce-scatter.12.cloned.1.call-update) | async-done | bytes 1572880 | tf_op jit(solution)/shard_map/reduce_scatter | solution.py:194
  618.9 45.0 %reduce-scatter.16.cloned.1.call-done = f32[96,768]{1,0:T(8,128)} async-done(((f32[768,768]{1,0:T(8,128)}), f32[96,768]{1,0:T(8,128)}) %reduce-scatter.16.cloned.1.call-update) | async-done | bytes 294928 | tf_op jit(solution)/shard_map/reduce_scatter | solution.py:219
  665.6 163.4 %reduce-scatter.18.cloned.1.call-done = f32[96,3072]{1,0:T(8,128)} async-done(((f32[768,3072]{1,0:T(8,128)}), f32[96,3072]{1,0:T(8,128)}) %reduce-scatter.18.cloned.1.call-update) | async-done | bytes 1179664 | tf_op jit(solution)/shard_map/reduce_scatter | solution.py:220
  831.1 162.6 %reduce-scatter.20.cloned.1.call-done = f32[384,768]{1,0:T(8,128)} async-done(((f32[3072,768]{1,0:T(8,128)}), f32[384,768]{1,0:T(8,128)}) %reduce-scatter.20.cloned.1.call-update) | async-done | bytes 1179664 | tf_op jit(solution)/shard_map/reduce_scatter | solution.py:221
  995.8 130.2 %reduce-scatter.22.cloned.1.call-done = f32[96,2304]{1,0:T(8,128)} async-done(((f32[768,2304]{1,0:T(8,128)}), f32[96,2304]{1,0:T(8,128)}) %reduce-scatter.22.cloned.1.call-update) | async-done | bytes 884752 | tf_op jit(solution)/shard_map/reduce_scatter | solution.py:218
  1137.3 53.7 %reduce-scatter.24.cloned.1.call-done = f32[96,12]{1,0:T(8,128)} async-done(((f32[768,12]{1,0:T(8,128)}), f32[96,12]{1,0:T(8,128)}) %reduce-scatter.24.cloned.1.call-update) | async-done | bytes 4624
  1198.2 42.3 %all-reduce.3.cloned.1.call-done = (bf16[96,2304]{1,0:T(8,128)(2,1)}, bf16[96,768]{1,0:T(8,128)(2,1)}, bf16[96,3072]{1,0:T(8,128)(2,1)}, bf16[384,768]{1,0:T(8,128)(2,1)}) async-done(((bf16[96,2304]{1,0:T(8,128)(2,1)}, bf16[96,768]{1,0:T(8,128)(2,1)}, bf16[96,3072]{1,0:T(8,128)(2,1)}, bf16[384,768]{1,0:T(8,128)(2,1)}), (bf16[96,2304]{1,0:T(8,128)(2,1)}, bf16[96,768]{1,0:T(8,128)(2,1)}, ...) | async-done | bytes 1769488 | tf_op jit(solution)/shard_map/psum | solution.py:225
  (205 shorter events, 243.7 us)
Async XLA Ops:
  7.2 135.3 %all-gather.9.cloned.1.call-start = ((), (), s32[]{:S(2)}) async-start(), calls=%async_computation.8 | async-start | bytes 7864320 | tf_op jit(solution)/shard_map/all_gather | solution.py:122
  10.3 21.9 %collective-permute-start = (bf16[96,2304]{1,0:T(8,128)(2,1)S(1)}, bf16[96,2304]{1,0:T(8,128)(2,1)S(1)}, u32[]{:S(2)}, u32[]{:S(2)}) collective-permute-start(bf16[96,2304]{1,0:T(8,128)(2,1)S(1)} %get-tuple-element.132), channel_id=1, source_target_pairs={{0,4},{4,8},{8,12},{12,16},{16,20},{20,24},{24,28},{28,0},{1,5},{5... | collective-permute-start | bytes 1327112 | tf_op jit(solution)/shard_map/ppermute | solution.py:28
  13.3 21.4 %collective-permute-start.1 = (bf16[96,2304]{1,0:T(8,128)(2,1)S(1)}, bf16[96,2304]{1,0:T(8,128)(2,1)S(1)}, u32[]{:S(2)}, u32[]{:S(2)}) collective-permute-start(bf16[96,2304]{1,0:T(8,128)(2,1)S(1)} %get-tuple-element.132), channel_id=1, source_target_pairs={{0,28},{4,0},{8,4},{12,8},{16,12},{20,16},{24,20},{28,24},{1,29},{... | collective-permute-start | bytes 1327112 | tf_op jit(solution)/shard_map/ppermute | solution.py:31
  16.3 70.3 %copy-start.38 = (bf16[8,128,768]{2,1,0:T(8,128)(2,1)S(1)}, bf16[8,128,768]{2,1,0:T(8,128)(2,1)}, u32[]{:S(2)}) copy-start(bf16[8,128,768]{2,1,0:T(8,128)(2,1)} %param.19) | copy-start | bytes 4718596
  32.2 20.5 %collective-permute-start.2 = (bf16[96,2304]{1,0:T(8,128)(2,1)S(1)}, bf16[96,2304]{1,0:T(8,128)(2,1)S(1)}, u32[]{:S(2)}, u32[]{:S(2)}) collective-permute-start(bf16[96,2304]{1,0:T(8,128)(2,1)S(1)} %collective-permute-done), channel_id=1, source_target_pairs={{0,4},{4,8},{8,12},{12,16},{16,20},{20,24},{24,28},{28,0},{1,5},{5... | collective-permute-start | bytes 1327112 | tf_op jit(solution)/shard_map/ppermute | solution.py:28
  34.6 20.5 %collective-permute-start.3 = (bf16[96,2304]{1,0:T(8,128)(2,1)S(1)}, bf16[96,2304]{1,0:T(8,128)(2,1)S(1)}, u32[]{:S(2)}, u32[]{:S(2)}) collective-permute-start(bf16[96,2304]{1,0:T(8,128)(2,1)S(1)} %collective-permute-done.1), channel_id=1, source_target_pairs={{0,28},{4,0},{8,4},{12,8},{16,12},{20,16},{24,20},{28,24},{1,29},{... | collective-permute-start | bytes 1327112 | tf_op jit(solution)/shard_map/ppermute | solution.py:31
  52.7 19.8 %collective-permute-start.4 = (bf16[96,2304]{1,0:T(8,128)(2,1)S(1)}, bf16[96,2304]{1,0:T(8,128)(2,1)S(1)}, u32[]{:S(2)}, u32[]{:S(2)}) collective-permute-start(bf16[96,2304]{1,0:T(8,128)(2,1)S(1)} %collective-permute-done.2), channel_id=1, source_target_pairs={{0,4},{4,8},{8,12},{12,16},{16,20},{20,24},{24,28},{28,0},{1,5},{5... | collective-permute-start | bytes 1327112 | tf_op jit(solution)/shard_map/ppermute | solution.py:28
  55.2 20.6 %collective-permute-start.5 = (bf16[96,2304]{1,0:T(8,128)(2,1)S(1)}, bf16[96,2304]{1,0:T(8,128)(2,1)S(1)}, u32[]{:S(2)}, u32[]{:S(2)}) collective-permute-start(bf16[96,2304]{1,0:T(8,128)(2,1)S(1)} %collective-permute-done.3), channel_id=1, source_target_pairs={{0,28},{4,0},{8,4},{12,8},{16,12},{20,16},{24,20},{28,24},{1,29},{... | collective-permute-start | bytes 1327112 | tf_op jit(solution)/shard_map/ppermute | solution.py:31
  72.5 13.3 %collective-permute-start.6 = (bf16[96,2304]{1,0:T(8,128)(2,1)S(1)}, bf16[96,2304]{1,0:T(8,128)(2,1)S(1)}, u32[]{:S(2)}, u32[]{:S(2)}) collective-permute-start(bf16[96,2304]{1,0:T(8,128)(2,1)S(1)} %collective-permute-done.4), channel_id=1, source_target_pairs={{0,4},{4,8},{8,12},{12,16},{16,20},{20,24},{24,28},{28,0},{1,5},{5... | collective-permute-start | bytes 1327112 | tf_op jit(solution)/shard_map/ppermute | solution.py:28
  97.4 93.6 %all-gather.7.cloned.1.call-start = ((), (), s32[]{:S(2)}) async-start(), calls=%async_computation.7 | async-start | bytes 7864320 | tf_op jit(solution)/shard_map/all_gather | solution.py:123
  133.5 101.4 %all-gather.11.cloned.1.call-start = ((), (), s32[]{:S(2)}) async-start(), calls=%async_computation.9 | async-start | bytes 1327104 | tf_op jit(solution)/shard_map/all_gather | solution.py:93
  134.3 181.3 %all-gather.13.cloned.1.call-start = ((), (), s32[]{:S(2)}) async-start(), calls=%async_computation.10 | async-start | bytes 5308416 | tf_op jit(solution)/shard_map/all_gather | solution.py:94
  135.2 260.7 %all-gather.15.cloned.1.call-start = ((), (), s32[]{:S(2)}) async-start(), calls=%async_computation.11 | async-start | bytes 5308416 | tf_op jit(solution)/shard_map/all_gather | solution.py:95
  137.5 433.1 %reduce-scatter.14.cloned.1.call-start = ((), (), s32[]{:S(2)}) async-start(), calls=%async_computation.13 | async-start | bytes 7864320 | tf_op jit(solution)/shard_map/reduce_scatter | solution.py:197
  315.6 80.3 %copy-start.36 = (f32[768]{0:T(1024)S(1)}, f32[768]{0:T(1024)}, u32[]{:S(2)}) copy-start(f32[768]{0:T(1024)} %get-tuple-element.95) | copy-start | bytes 9220
  472.1 118.8 %reduce-scatter.12.cloned.1.call-start = ((), (), s32[]{:S(2)}) async-start(), calls=%async_computation.12 | async-start | bytes 7864320 | tf_op jit(solution)/shard_map/reduce_scatter | solution.py:194
  528.5 135.5 %reduce-scatter.16.cloned.1.call-start = ((), (), s32[]{:S(2)}) async-start(), calls=%async_computation.14 | async-start | bytes 2654208 | tf_op jit(solution)/shard_map/reduce_scatter | solution.py:219
  533.9 295.0 %reduce-scatter.18.cloned.1.call-start = ((), (), s32[]{:S(2)}) async-start(), calls=%async_computation.15 | async-start | bytes 10616832 | tf_op jit(solution)/shard_map/reduce_scatter | solution.py:220
  544.8 448.9 %reduce-scatter.20.cloned.1.call-start = ((), (), s32[]{:S(2)}) async-start(), calls=%async_computation.16 | async-start | bytes 10616832 | tf_op jit(solution)/shard_map/reduce_scatter | solution.py:221
  557.6 568.4 %reduce-scatter.22.cloned.1.call-start = ((), (), s32[]{:S(2)}) async-start(), calls=%async_computation.17 | async-start | bytes 7962624 | tf_op jit(solution)/shard_map/reduce_scatter | solution.py:218
  610.3 580.7 %reduce-scatter.24.cloned.1.call-start = ((), (), s32[]{:S(2)}) async-start(), calls=%async_computation.18 | async-start | bytes 442368
  618.0 622.5 %all-reduce.3.cloned.1.call-start = ((), (), s32[]{:S(2)}) async-start(), calls=%async_computation.19 | async-start | bytes 3538944 | tf_op jit(solution)/shard_map/psum | solution.py:225
  665.6 462.4 %copy-start.6 = (f32[1024,768]{1,0:T(8,128)S(1)}, f32[1024,768]{1,0:T(8,128)}, u32[]{:S(2)}) copy-start(f32[1024,768]{1,0:T(8,128)} %copy-done.5) | copy-start | bytes 9437188
  1128.0 112.4 %copy-start.23 = (f32[96,768]{1,0:T(8,128)S(1)}, f32[96,768]{1,0:T(8,128)}, u32[]{:S(2)}) copy-start(f32[96,768]{1,0:T(8,128)} %param.24) | copy-start | bytes 884740
  (36 other events, 449.3 us)
Sparse Core Ops, SparseCore 0:
  97.5 44.8 all-gather.8
  144.6 46.3 all-gather.6
  193.8 41.1 all-gather.10
  237.5 77.9 all-gather.12
  318.2 77.6 all-gather.14
  472.2 57.2 reduce-scatter.13
  532.0 58.8 reduce-scatter.11
  594.4 69.5 reduce-scatter.15
  667.5 161.3 reduce-scatter.17
  832.4 161.2 reduce-scatter.19
  997.4 128.5 reduce-scatter.21
  1129.7 61.2 reduce-scatter.23
  1195.3 45.1 all-reduce.2
